TPU v7x, 768 devices: a whole 4x8x12 slice. The times are simulated.
768 devices in a mesh: blk: 192 (over y, z, core), grp: 4 (over x).
Axes of the slice: x: 4, y: 8, z: 12, core: 2. Of those that a mesh axis runs over, the one named last changes fastest.
Arguments:
- dual_rhs: float32 [4, 16, 196608], P('grp', None, 'blk'), may hold values from -32 to 32
- dual_ops: bfloat16 [4, 196608, 1024], P('grp', 'blk'), may hold values from -1 to 6, as said below
- prec_ops: bfloat16 [4, 196608, 1024], P('grp', 'blk'), may hold values from -1 to 4, as said below
- corner_coupling: bfloat16 [4, 4608, 512], P('grp', 'blk'), may hold values from -0.25 to 0.25
- corner_map: int32 [4, 4608], P('grp', 'blk'), may hold values from 0 to 767
- signs: int32 [4, 196608], P('grp', 'blk'), may hold values from -1 to 1, as said below
- coarse_inverse: float32 [768, 768], replicated, may hold values from -1 to 5, as said below
Outputs:
- multipliers: float32 [4, 16, 196608], P('grp', None, 'blk')
- residual: float32 [4, 16, 196608], P('grp', None, 'blk')
Inputs may be any that keep to these rules, and one draw needn't show every extreme that they name: `dual_ops`: each subdomain's 1024 x 1024 block is symmetric positive definite. `prec_ops`: each subdomain's 1024 x 1024 block is symmetric positive definite. `signs`: every entry is 1 or -1; the lower face of each subdomain after the first of a group carries the negated signs of the upper face of the subdomain before it. `coarse_inverse`: symmetric positive definite.
All inputs are finite; a program needn't handle non-finite values.
Results may differ from a plain program's by a relative error of at most 0.003.
Values sent between devices are 32-bit elements; how exact they have to be, the bound alone decides.
A program may use at most 32 MiB of HBM per device.

v0:
```python
import jax
import jax.numpy as jnp
from jax import lax
from jax.sharding import PartitionSpec as P

ITERS = 2


def extended(block, sides, width):
    for axis, dim in sides:
        count = lax.axis_size(axis)
        forward = [(i, i + 1) for i in range(count - 1)]
        backward = [(target, source) for source, target in forward]
        low = lax.ppermute(
            lax.slice_in_dim(block, block.shape[dim] - width, None, axis=dim), axis, forward
        )
        high = lax.ppermute(lax.slice_in_dim(block, 0, width, axis=dim), axis, backward)
        block = jnp.concatenate([low, block, high], axis=dim)
    return block


def gram_solve(matrix, target):
    balanced = 0.5 * (matrix + matrix.T)
    factor = jnp.linalg.cholesky(balanced)
    middle = lax.linalg.triangular_solve(factor, target, left_side=True, lower=True)
    return lax.linalg.triangular_solve(factor, middle, left_side=True, lower=True, transpose_a=True)


def local(dual_rhs, dual_ops, prec_ops, corner_coupling, corner_map, signs, coarse_inverse):
    highest = lax.Precision.HIGHEST
    width = dual_rhs.shape[2]
    face_width = width // 2
    blk_index = lax.axis_index("blk")
    blk_count = lax.axis_size("blk")
    lower_live = jnp.where(blk_index > 0, 1.0, 0.0).astype(jnp.float32)
    upper_live = jnp.where(blk_index < blk_count - 1, 1.0, 0.0).astype(jnp.float32)
    live_face = jnp.concatenate(
        [
            jnp.full((face_width,), 1.0, jnp.float32) * lower_live,
            jnp.full((face_width,), 1.0, jnp.float32) * upper_live,
        ]
    )
    face_sign = signs[0].astype(jnp.float32) * live_face
    couple = corner_coupling[0].astype(jnp.float32)
    corner_rows = couple.shape[0] // 2
    couple_lower = couple[:corner_rows]
    couple_upper = couple[corner_rows:]
    corners = coarse_inverse.shape[0]
    onehot = (corner_map[0][:, None] == jnp.arange(corners, dtype=jnp.int32)[None, :]).astype(
        jnp.float32
    )
    contract_last = (((1,), (1,)), ((), ()))
    contract_first = (((0,), (0,)), ((), ()))

    def assemble(local_out):
        signed_out = face_sign * local_out
        beside_all = extended(signed_out, (("blk", 1),), face_width)
        partner = jnp.concatenate(
            [beside_all[:, :face_width], beside_all[:, face_width + width :]], axis=1
        )
        return live_face * (signed_out + partner)

    def local_product(signed_in, blocks):
        rounded = signed_in.astype(jnp.bfloat16)
        return lax.dot_general(
            rounded, blocks[0], contract_last, preferred_element_type=jnp.float32
        )

    def corner_terms(values):
        signed_in = face_sign * values
        lower_part = lax.dot_general(
            signed_in[:, :face_width], couple_lower, contract_last, precision=highest
        )
        upper_part = lax.dot_general(
            signed_in[:, face_width:], couple_upper, contract_last, precision=highest
        )
        partial_value = jnp.concatenate([lower_part, upper_part], axis=1)
        return jnp.dot(partial_value, onehot, precision=highest)

    def precondition(values):
        return assemble(local_product(face_sign * values, prec_ops))

    def region(values):
        return lax.psum(values, ("blk", "grp"))

    def sectioned(values):
        within = lax.psum(values, "blk")
        return lax.psum(within, "grp")

    def gram_of(first, second):
        return lax.dot_general(first, second, contract_last, precision=highest)

    def combine(weights, values):
        return lax.dot_general(weights, values, contract_first, precision=highest)

    residual = live_face * dual_rhs[0]
    multipliers = jnp.zeros_like(residual)
    precond = precondition(residual)
    gram_old = region(gram_of(residual, precond))
    corner_sum = sectioned(corner_terms(precond))
    direction = precond
    for iteration in range(ITERS):
        solved = lax.dot_general(corner_sum, coarse_inverse, contract_last, precision=highest)
        picked = lax.dot_general(solved, onehot, contract_last, precision=highest)
        lower_out = jnp.dot(picked[:, :corner_rows], couple_lower, precision=highest)
        upper_out = jnp.dot(picked[:, corner_rows:], couple_upper, precision=highest)
        image_dir = assemble(
            local_product(face_sign * direction, dual_ops)
            + jnp.concatenate([lower_out, upper_out], axis=1)
        )
        step_alpha = gram_solve(region(gram_of(direction, image_dir)), gram_old)
        multipliers = multipliers + combine(step_alpha, direction)
        residual = residual - combine(step_alpha, image_dir)
        if iteration + 1 < ITERS:
            precond = precondition(residual)
            gram_new = region(gram_of(residual, precond))
            step_beta = gram_solve(gram_old, gram_new)
            direction = precond + combine(step_beta, direction)
            corner_sum = sectioned(corner_terms(direction))
            gram_old = gram_new
    return (multipliers[None], residual[None])


def solution(mesh):
    in_specs = (
        P("grp", None, "blk"),
        P("grp", "blk", None),
        P("grp", "blk", None),
        P("grp", "blk", None),
        P("grp", "blk"),
        P("grp", "blk"),
        P(),
    )
    out_specs = (P("grp", None, "blk"), P("grp", None, "blk"))
    return jax.shard_map(local, mesh=mesh, in_specs=in_specs, out_specs=out_specs, check_vma=False)
```

profile of v0, /device:TPU:1, one launch (start us, length us, event | category | flops | bytes accessed | tf_op | source)
XLA Modules:
  0.0 1907.4 jit_solution(10213638809837328328)
XLA Ops:
  0.7 0.8 convert_element_type.23
  1.5 2.3 fusion.8
  3.8 5.4 collective-permute-start
  9.2 8.3 collective-permute-start.1
  17.5 0.8 collective-permute-done.1
  18.4 0.1 fusion.49
  18.5 0.1 fusion.47
  18.7 0.2 fusion.31
  18.9 737.3 %psum.56 = f32[16,768]{1,0:T(8,128)S(1)} all-reduce(f32[16,768]{1,0:T(8,128)S(1)} %fusion.31), channel_id=1, replica_groups=mesh['blk'=192,'grp'=4] {'blk'}, use_global_device_ids=true, to_apply=%region_0.1 | all-reduce | flops 12288 | bytes 98304 | tf_op jit(solution)/shard_map/psum | solution.py:87
  756.2 13.7 psum.57
  769.9 2.0 fusion.129
  771.9 0.2 fusion.30
  772.1 0.2 fusion.60
  772.3 0.1 fusion.66
  772.5 0.6 fusion.17
  773.2 7.3 collective-permute-start.2
  780.5 5.2 collective-permute-start.3
  785.8 0.2 fusion.36
  786.0 0.6 collective-permute-done.3
  786.6 0.2 fusion.70
  786.8 110.4 %all-reduce.1 = (f32[16,16]{1,0:T(8,128)S(1)}, f32[16,16]{1,0:T(8,128)S(1)}) all-reduce(f32[16,16]{1,0:T(8,128)S(1)} %fusion.36, f32[16,16]{1,0:T(8,128)S(1)} %fusion.70), channel_id=1, replica_groups=mesh['blk'=192,'grp'=4] {'blk','grp'}, use_global_device_ids=true, to_apply=%region_5.7 | all-reduce | flops 512 | bytes 4096 | tf_op jit(solution)/shard_map/psum | solution.py:84
  897.4 1.5 cholesky.70
  898.9 0.6 compare_reduce_fusion.1
  899.6 1.5 cholesky.59
  901.1 0.6 compare_reduce_fusion.2
  901.7 0.6 fusion.85
  902.4 1.2 custom-call.13
  903.6 0.2 fusion.110
  903.8 0.1 fusion.112
  904.0 0.3 convolution_subtract_fusion.1
  904.2 2.2 fusion.11
  906.5 2.2 collective-permute-start.4
  908.7 2.1 collective-permute-start.5
  910.8 0.7 fusion.86
  911.5 1.2 custom-call.15
  912.7 1.2 collective-permute-done.5
  914.0 0.2 fusion.75
  914.1 112.3 %psum.60 = f32[16,16]{1,0:T(8,128)S(1)} all-reduce(f32[16,16]{1,0:T(8,128)S(1)} %fusion.75), channel_id=1, replica_groups=mesh['blk'=192,'grp'=4] {'blk','grp'}, use_global_device_ids=true, to_apply=%region_6.10 | all-reduce | flops 256 | bytes 2048 | tf_op jit(solution)/shard_map/psum | solution.py:84
  1026.4 0.2 fusion.104
  1026.6 0.1 fusion.106
  1026.8 0.3 broadcast_multiply_fusion
  1027.2 0.1 fusion.43
  1027.3 0.2 fusion.29
  1027.6 732.0 %psum.61 = f32[16,768]{1,0:T(8,128)S(1)} all-reduce(f32[16,768]{1,0:T(8,128)S(1)} %fusion.29), channel_id=1, replica_groups=mesh['blk'=192,'grp'=4] {'blk'}, use_global_device_ids=true, to_apply=%region_7.11 | all-reduce | flops 12288 | bytes 98304 | tf_op jit(solution)/shard_map/psum | solution.py:87
  1759.6 12.1 psum.62
  1771.7 2.0 fusion.130
  1773.7 0.2 fusion.28
  1773.9 0.2 fusion.57
  1774.2 0.1 fusion.63
  1774.4 0.6 fusion.23
  1775.0 7.3 collective-permute-start.6
  1782.4 5.2 collective-permute-start.7
  1787.6 0.8 collective-permute-done.7
  1788.5 0.2 fusion.73
  1788.6 112.2 %psum.63 = f32[16,16]{1,0:T(8,128)S(1)} all-reduce(f32[16,16]{1,0:T(8,128)S(1)} %fusion.73), channel_id=1, replica_groups=mesh['blk'=192,'grp'=4] {'blk','grp'}, use_global_device_ids=true, to_apply=%region_9.13 | all-reduce | flops 256 | bytes 2048 | tf_op jit(solution)/shard_map/psum | solution.py:84
  1901.0 1.5 cholesky.81
  1902.5 0.6 compare_reduce_fusion
  1903.2 0.6 fusion.87
  1903.8 1.2 custom-call.17
  1905.0 0.2 fusion.98
  1905.2 0.1 fusion.100
  1905.4 0.3 fusion.131
  1905.7 0.9 fusion.27
  1906.5 0.9 fusion.26
  (38 shorter events, 0.8 us)
Async XLA Ops:
  0.6 769.2 %copy-start = (f32[768,768]{1,0:T(8,128)S(1)}, f32[768,768]{1,0:T(8,128)}, u32[]{:S(2)}) copy-start(f32[768,768]{1,0:T(8,128)} %param.18) | copy-start | bytes 7077892
  0.6 17.7 copy-start.4
  0.7 18.0 copy-start.5
  3.8 13.7 collective-permute-start
  9.2 9.1 collective-permute-start.1
  769.9 2.6 copy-start.1
  769.9 15.9 copy-start.3
  773.2 12.8 collective-permute-start.2
  780.5 6.1 collective-permute-start.3
  906.5 6.2 collective-permute-start.4
  908.7 5.2 collective-permute-start.5
  1771.7 2.6 copy-start.2
  1775.0 12.6 collective-permute-start.6
  1782.4 6.1 collective-permute-start.7
where the time goes:
time: 1910 us
  blocking collectives  1830 us (96%)
  starting transfers between devices  43.1 us (2%)
    psum x2, blocking collectives, sectioned(): within = lax.psum(values, 'blk')  1470 us
    psum x3, blocking collectives, region(): return lax.psum(values, ('blk', 'grp'))  335 us
  transfers between devices with their start and end apart: 8, of which 4 were waited for; matrix products, arithmetic and copies ran while one was open for 0% of the time, Pallas kernels for 0%

commit v1 on v0

v1 whole, which is shorter than its diff:
```python
import functools

import jax
import jax.numpy as jnp
from jax import lax
from jax.experimental import pallas as pl
from jax.experimental.pallas import tpu as pltpu
from jax.sharding import PartitionSpec as P

F32 = jnp.float32
BF16 = jnp.bfloat16
HIGHEST = lax.Precision.HIGHEST
LAST = (((1,), (1,)), ((), ()))
PLAIN = (((1,), (0,)), ((), ()))
FIRST = (((0,), (0,)), ((), ()))
NRHS = 16
HALF = 512
WIDTH = 2 * HALF
FACE_CORNERS = 12
CORNERS = 768
PAYLOAD = 1024


def split(value, terms):
    parts = []
    for _ in range(terms):
        part = value.astype(BF16)
        parts.append(part)
        value = value - part.astype(F32)
    return parts


def narrow_dot(value, exact, dims, terms=3):
    rows = value.shape[0]
    stacked = jnp.concatenate(split(value, terms), axis=0)
    out = lax.dot_general(stacked, exact, dims, preferred_element_type=F32)
    total = out[:rows]
    for term in range(1, terms):
        total = total + out[term * rows : (term + 1) * rows]
    return total


def full_dot(left, right, dims):
    return lax.dot_general(left, right, dims, precision=HIGHEST, preferred_element_type=F32)


def symmetric_part(matrix):
    return 0.5 * (matrix + matrix.T)


def spd_solve(matrix, target):
    size = matrix.shape[0]
    both = jnp.concatenate([matrix, target], axis=1)
    rows = lax.broadcasted_iota(jnp.int32, both.shape, 0)
    for k in range(size):
        column = jnp.broadcast_to(both[:, k : k + 1], both.shape)
        pivot_row = both[k : k + 1, :] / column[k : k + 1, :]
        both = jnp.where(rows == k, pivot_row, both - column * pivot_row)
    return both[:, size:]


def kernel(
    blk_count, grp_count, ny, nz,
    rhs_ref, prec_hbm, dual_hbm, couple_ref, map_ref, sign_ref, inverse_hbm,
    mult_ref, resid_ref,
    prec, dual, inverse, inverse_high, inverse_low,
    face_out, face_in, pieces, gathered, by_y, by_z, final,
    load_sem, face_send, face_recv,
    scatter_send, scatter_recv, y_send, y_recv, z_send, z_recv, final_send, final_recv,
):
    loads = [
        pltpu.make_async_copy(source, target, load_sem.at[index])
        for index, (source, target) in enumerate(
            ((prec_hbm, prec), (dual_hbm, dual), (inverse_hbm, inverse))
        )
    ]
    for load in loads:
        load.start()

    blk = lax.axis_index("blk")
    grp = lax.axis_index("grp")
    core = lax.rem(blk, 2)
    z = lax.rem(lax.div(blk, 2), nz)
    y = lax.div(blk, 2 * nz)
    spot = grp * 2 + core
    spots = 2 * grp_count
    lanes = PAYLOAD // spots

    def at(blk_index, grp_index):
        return {"blk": blk_index, "grp": grp_index}

    def spot_peer(step):
        other = lax.rem(spot + step, spots)
        return other, at(blk - core + lax.rem(other, 2), lax.div(other, 2))

    def y_peer(step):
        other = lax.rem(y + step, ny)
        return other, at(blk + (other - y) * (2 * nz), grp)

    def z_peer(step):
        other = lax.rem(z + step, nz)
        return other, at(blk + (other - z) * 2, grp)

    left = at(lax.rem(blk + blk_count - 1, blk_count), grp)
    right = at(lax.rem(blk + 1, blk_count), grp)

    barrier = pltpu.get_barrier_semaphore()
    greeted = [left, right]
    greeted += [spot_peer(step)[1] for step in range(1, spots)]
    greeted += [y_peer(step)[1] for step in range(1, ny)]
    greeted += [z_peer(step)[1] for step in range(1, nz)]
    for peer in greeted:
        pl.semaphore_signal(
            barrier, inc=1, device_id=peer, device_id_type=pl.DeviceIdType.MESH
        )

    def remote(source, target, send_sem, recv_sem, peer):
        return pltpu.make_async_remote_copy(
            src_ref=source,
            dst_ref=target,
            send_sem=send_sem,
            recv_sem=recv_sem,
            device_id=peer,
            device_id_type=pl.DeviceIdType.MESH,
        )

    def face_copies(turn):
        return (
            remote(
                face_out.at[turn, 0], face_in.at[turn, 1],
                face_send.at[turn, 0], face_recv.at[turn, 1], left,
            ),
            remote(
                face_out.at[turn, 1], face_in.at[turn, 0],
                face_send.at[turn, 1], face_recv.at[turn, 0], right,
            ),
        )

    def send_faces(turn, signed_out):
        face_out[turn, 0] = signed_out[:, :HALF]
        face_out[turn, 1] = signed_out[:, HALF:]
        for copy in face_copies(turn):
            copy.start()

    def take_faces(turn, signed_out):
        for copy in face_copies(turn):
            copy.wait_recv()
        partner = jnp.concatenate([face_in[turn, 0], face_in[turn, 1]], axis=1)
        return live * (signed_out + partner)

    def group_copies(peer_of, count, own, source_of, buffer, send_sem, recv_sem):
        copies = []
        for step in range(1, count):
            other, peer = peer_of(step)
            send = remote(source_of(other), buffer.at[own], send_sem.at[other], recv_sem.at[own], peer)
            recv = remote(source_of(other), buffer.at[other], send_sem.at[other], recv_sem.at[other], peer)
            copies.append((send, recv))
        return copies

    def start_all(copies):
        for send, _ in copies:
            send.start()

    def finish_all(copies):
        for _, recv in copies:
            recv.wait_recv()

    def drain_all(copies):
        for send, _ in copies:
            send.wait_send()

    def total_of(buffer, turn, count):
        total = buffer[turn, 0]
        for index in range(1, count):
            total = total + buffer[turn, index]
        return total

    def reduce_all(turn, payload, meanwhile):
        for index in range(spots):
            pieces[turn, index] = payload[:, index * lanes : (index + 1) * lanes]
        scatter = group_copies(
            spot_peer, spots, spot, lambda other: pieces.at[turn, other],
            gathered.at[turn], scatter_send.at[turn], scatter_recv.at[turn],
        )
        start_all(scatter)
        gathered[turn, spot] = pieces[turn, spot]
        between = meanwhile()
        finish_all(scatter)
        by_y[turn, y] = total_of(gathered, turn, spots)
        along_y = group_copies(
            y_peer, ny, y, lambda other: by_y.at[turn, y],
            by_y.at[turn], y_send.at[turn], y_recv.at[turn],
        )
        start_all(along_y)
        finish_all(along_y)
        by_z[turn, z] = total_of(by_y, turn, ny)
        along_z = group_copies(
            z_peer, nz, z, lambda other: by_z.at[turn, z],
            by_z.at[turn], z_send.at[turn], z_recv.at[turn],
        )
        start_all(along_z)
        finish_all(along_z)
        final[turn, spot] = total_of(by_z, turn, nz)
        spread = group_copies(
            spot_peer, spots, spot, lambda other: final.at[turn, spot],
            final.at[turn], final_send.at[turn], final_recv.at[turn],
        )
        start_all(spread)
        finish_all(spread)
        reduced = jnp.concatenate([final[turn, index] for index in range(spots)], axis=1)
        for copies in (scatter, along_y, along_z, spread):
            drain_all(copies)
        grams = [
            reduced[:, CORNERS + NRHS * index : CORNERS + NRHS * (index + 1)] for index in range(3)
        ]
        return reduced[:, :CORNERS], grams, between

    def pack(corner, grams):
        zeros = jnp.zeros((NRHS, PAYLOAD - CORNERS - NRHS * len(grams)), F32)
        return jnp.concatenate([corner, *grams, zeros], axis=1)

    lane = lax.broadcasted_iota(jnp.int32, (1, WIDTH), 1)
    lower_live = jnp.where(blk > 0, 1.0, 0.0).astype(F32)
    upper_live = jnp.where(blk < blk_count - 1, 1.0, 0.0).astype(F32)
    live = jnp.where(lane < HALF, lower_live, upper_live)
    face_sign = sign_ref[...].astype(F32) * live

    rows = 2 * FACE_CORNERS
    couple = couple_ref[0].astype(F32)
    couple_row = lax.broadcasted_iota(jnp.int32, couple.shape, 0)
    coupling = jnp.concatenate(
        [
            jnp.where(couple_row < FACE_CORNERS, couple, 0.0),
            jnp.where(couple_row >= FACE_CORNERS, couple, 0.0),
        ],
        axis=1,
    ).astype(BF16)
    diagonal = lax.broadcasted_iota(jnp.int32, (rows, rows), 0) == lax.broadcasted_iota(
        jnp.int32, (rows, rows), 1
    )
    map_row = jnp.broadcast_to(map_ref[...].astype(F32), (rows, rows))
    map_column = jnp.sum(jnp.where(diagonal, map_row, 0.0), axis=1, keepdims=True)
    corner_lane = lax.broadcasted_iota(jnp.int32, (rows, CORNERS), 1).astype(F32)
    onehot = jnp.where(map_column == corner_lane, 1.0, 0.0).astype(BF16)

    def local_product(values, blocks):
        return lax.dot_general(
            (face_sign * values).astype(BF16), blocks[...], PLAIN, preferred_element_type=F32
        )

    def corner_terms(values):
        partial = narrow_dot(face_sign * values, coupling, LAST)
        return narrow_dot(partial, onehot, PLAIN)

    def combine(weights, values):
        return full_dot(weights.T, values, PLAIN)

    residual = live * rhs_ref[0]
    loads[0].wait()
    signed_out = face_sign * local_product(residual, prec)
    pl.semaphore_wait(barrier, len(greeted))
    send_faces(0, signed_out)
    loads[1].wait()
    direction = take_faces(0, signed_out)
    corner = corner_terms(direction)
    image_local = local_product(direction, dual)
    payload = pack(
        corner,
        [
            full_dot(residual, direction, LAST),
            2.0 * full_dot(face_sign * direction, image_local, LAST),
        ],
    )

    def prepare():
        loads[2].wait()
        high, middle, low = split(inverse[...], 3)
        inverse_high[...] = high
        inverse_low[...] = middle
        picked = lax.dot_general(onehot, high, PLAIN, preferred_element_type=F32)
        picked = picked + lax.dot_general(onehot, middle, PLAIN, preferred_element_type=F32)
        return picked + lax.dot_general(onehot, low, PLAIN, preferred_element_type=F32)

    corner_old, (gram_old, curve_local, _), inverse_rows = reduce_all(0, payload, prepare)

    def solve_corners(values):
        high, low = split(values, 2)
        both = lax.dot_general(
            jnp.concatenate([high, low], axis=0), inverse_high[...], PLAIN,
            preferred_element_type=F32,
        )
        cross = lax.dot_general(high, inverse_low[...], PLAIN, preferred_element_type=F32)
        return both[:NRHS] + (both[NRHS:] + cross)

    picked_old = full_dot(corner_old, inverse_rows, LAST)
    signed_out = face_sign * (image_local + narrow_dot(picked_old, coupling, PLAIN))
    send_faces(1, signed_out)
    solved_old = solve_corners(corner_old)
    curve_old = curve_local + 2.0 * full_dot(corner_old, solved_old, LAST)
    curve_old = symmetric_part(curve_old)
    alpha = spd_solve(curve_old, gram_old)
    image_dir = take_faces(1, signed_out)
    residual = residual - combine(alpha, image_dir)
    signed_out = face_sign * local_product(residual, prec)
    send_faces(2, signed_out)
    multipliers = combine(alpha, direction)
    precond = take_faces(2, signed_out)
    corner = corner_terms(precond)
    precond_local = local_product(precond, dual)
    signed_precond = face_sign * precond
    payload = pack(
        corner,
        [
            full_dot(residual, precond, LAST),
            2.0 * full_dot(signed_precond, precond_local, LAST),
            2.0 * full_dot(signed_precond, image_local, LAST),
        ],
    )

    def invert():
        unit = lax.broadcasted_iota(jnp.int32, (NRHS, NRHS), 0) == lax.broadcasted_iota(
            jnp.int32, (NRHS, NRHS), 1
        )
        return spd_solve(symmetric_part(gram_old), jnp.where(unit, 1.0, 0.0).astype(F32))

    corner_new, (gram_new, curve_new, cross), gram_inverse = reduce_all(1, payload, invert)
    beta = full_dot(gram_inverse, gram_new, PLAIN)
    direction = precond + combine(beta, direction)
    picked = full_dot(corner_new, inverse_rows, LAST) + combine(beta, picked_old)
    signed_out = face_sign * (
        local_product(direction, dual) + narrow_dot(picked, coupling, PLAIN)
    )
    send_faces(3, signed_out)
    solved_new = solve_corners(corner_new)
    curve_new = curve_new + 2.0 * full_dot(corner_new, solved_new, LAST)
    cross = cross + 2.0 * full_dot(corner_new, solved_old, LAST)
    mixed = full_dot(cross, beta, PLAIN)
    quadratic = full_dot(beta.T, full_dot(curve_old, beta, PLAIN), PLAIN)
    curve = symmetric_part(curve_new + 2.0 * mixed + quadratic)
    alpha = spd_solve(curve, gram_new)
    mult_ref[0] = multipliers + combine(alpha, direction)
    image_dir = take_faces(3, signed_out)
    resid_ref[0] = residual - combine(alpha, image_dir)
    for turn in range(4):
        for copy in face_copies(turn):
            copy.wait_send()


def extents(blk_count):
    return {192: (8, 12), 8: (2, 2)}[blk_count]


def solution(mesh):
    blk_count, grp_count = mesh.shape["blk"], mesh.shape["grp"]
    ny, nz = extents(blk_count)
    spots = 2 * grp_count
    piece = (NRHS, PAYLOAD // spots)
    dma = pltpu.SemaphoreType.DMA
    in_vmem = pl.BlockSpec(memory_space=pltpu.VMEM)
    in_place = pl.BlockSpec(memory_space=pl.ANY)

    def local(dual_rhs, dual_ops, prec_ops, corner_coupling, corner_map, signs, coarse_inverse):
        result = jax.ShapeDtypeStruct((1, NRHS, WIDTH), F32)
        return pl.pallas_call(
            functools.partial(kernel, blk_count, grp_count, ny, nz),
            out_shape=(result, result),
            in_specs=[in_vmem, in_place, in_place, in_vmem, in_vmem, in_vmem, in_place],
            out_specs=(in_vmem, in_vmem),
            scratch_shapes=[
                pltpu.VMEM((WIDTH, WIDTH), BF16),
                pltpu.VMEM((WIDTH, WIDTH), BF16),
                pltpu.VMEM((CORNERS, CORNERS), F32),
                pltpu.VMEM((CORNERS, CORNERS), BF16),
                pltpu.VMEM((CORNERS, CORNERS), BF16),
                pltpu.VMEM((4, 2, NRHS, HALF), F32),
                pltpu.VMEM((4, 2, NRHS, HALF), F32),
                pltpu.VMEM((2, spots, *piece), F32),
                pltpu.VMEM((2, spots, *piece), F32),
                pltpu.VMEM((2, ny, *piece), F32),
                pltpu.VMEM((2, nz, *piece), F32),
                pltpu.VMEM((2, spots, *piece), F32),
                dma((3,)),
                dma((4, 2)),
                dma((4, 2)),
                dma((2, spots)),
                dma((2, spots)),
                dma((2, ny)),
                dma((2, ny)),
                dma((2, nz)),
                dma((2, nz)),
                dma((2, spots)),
                dma((2, spots)),
            ],
            compiler_params=pltpu.CompilerParams(
                collective_id=0, has_side_effects=True, vmem_limit_bytes=48 * 1024 * 1024
            ),
            name="block_conjugate_gradients",
        )(
            dual_rhs, prec_ops.reshape(WIDTH, WIDTH), dual_ops.reshape(WIDTH, WIDTH),
            corner_coupling, corner_map, signs, coarse_inverse,
        )

    in_specs = (
        P("grp", None, "blk"),
        P("grp", "blk", None),
        P("grp", "blk", None),
        P("grp", "blk", None),
        P("grp", "blk"),
        P("grp", "blk"),
        P(),
    )
    out_specs = (P("grp", None, "blk"), P("grp", None, "blk"))
    return jax.shard_map(local, mesh=mesh, in_specs=in_specs, out_specs=out_specs, check_vma=False)
```

time: 1910 us -> 87.6 us (0.05)
  blocking collectives: 1830 us -> 0 us
  Pallas kernels: 0 us -> 79.2 us
  starting transfers between devices: 43.1 us -> 0 us
    psum x7 -> x0, blocking collectives: 1830 us -> none  [the longest x2 1470 us: sectioned(): within = lax.psum(values, 'blk')]
    pallas_call x0 -> x1, Pallas kernels: none -> 79.2 us  [local(): pl.pallas_call(functools.partial(kernel, blk_count, grp_count, ny, nz), o...]
    ppermute x8 -> x0, starting transfers between devices: 43.1 us -> none  [the longest x4 22.3 us: extended(): lax.ppermute(lax.slice_in_dim(block, block.shape[dim] - width, None, axis...]
  transfers between devices with their start and end apart: 8 -> 0, of which waited for: 4 -> 0; matrix products, arithmetic and copies ran while one was open for 0% -> 0% of each run, Pallas kernels for 0% -> 0%
where the time goes in v1:
time: 87.6 us; the launch traced here: 87.2 us
  Pallas kernels  79.2 us (90%)
  local copies, waits for them, and re-layouts  7.35 us (8%)
    pallas_call x1, Pallas kernels, local(): pl.pallas_call(functools.partial(kernel, blk_count, grp_count, ny, nz), o...  79.2 us
    unnamed x14, local copies, waits for them, and re-layouts  7.35 us

profile of v1, /device:TPU:1, one launch (start us, length us, event | category | flops | bytes accessed | tf_op | source)
XLA Modules:
  0.0 87.2 jit_solution(5355285297429979680)
XLA Ops:
  0.6 0.0 copy-start
  0.6 1.6 %copy-done = bf16[1,1024,1024]{2,1,0:T(8,128)(2,1)S(1)} copy-done((bf16[1,1024,1024]{2,1,0:T(8,128)(2,1)S(1)}, bf16[1,1024,1024]{2,1,0:T(8,128)(2,1)}, u32[]{:S(2)}) %copy-start) | copy-done | bytes 2097176
  2.2 0.0 copy-start.1
  2.2 1.6 %copy-done.1 = bf16[1,1024,1024]{2,1,0:T(8,128)(2,1)S(1)} copy-done((bf16[1,1024,1024]{2,1,0:T(8,128)(2,1)S(1)}, bf16[1,1024,1024]{2,1,0:T(8,128)(2,1)}, u32[]{:S(2)}) %copy-start.1) | copy-done | bytes 2097176
  3.8 0.0 copy-start.2
  3.8 0.8 copy-done.2
  4.7 0.0 copy-start.3
  4.7 0.7 copy-done.3
  5.4 0.0 copy-start.4
  5.4 0.7 copy-done.4
  6.1 0.0 copy-start.5
  6.1 0.7 copy-done.5
  6.7 79.2 %block_conjugate_gradients.1 = (f32[1,16,1024]{2,1,0:T(8,128)S(1)}, f32[1,16,1024]{2,1,0:T(8,128)S(1)}) custom-call(f32[1,16,1024]{2,1,0:T(8,128)S(1)} %copy-done.2, bf16[1024,1024]{1,0:T(8,128)(2,1)S(1)} %bitcast.2, bf16[1024,1024]{1,0:T(8,128)(2,1)S(1)} %bitcast.3, bf16[1,24,512]{2,1,0:T(8,128)(2,1)S(1)} %copy-done.3, s32[1,24]{1,0:T(1,128)S(1)} %copy-done.5, ...), custom_call_target="tpu_custom_call" | custom-call | tf_op jit(solution)/shard_map/block_conjugate_gradients/pallas_call | solution.py:364
  85.9 0.6 copy.11
  86.5 0.6 copy.12
Async XLA Ops:
  0.6 1.6 %copy-start = (bf16[1,1024,1024]{2,1,0:T(8,128)(2,1)S(1)}, bf16[1,1024,1024]{2,1,0:T(8,128)(2,1)}, u32[]{:S(2)}) copy-start(bf16[1,1024,1024]{2,1,0:T(8,128)(2,1)} %param.9) | copy-start | bytes 6291460
  2.2 1.6 %copy-start.1 = (bf16[1,1024,1024]{2,1,0:T(8,128)(2,1)S(1)}, bf16[1,1024,1024]{2,1,0:T(8,128)(2,1)}, u32[]{:S(2)}) copy-start(bf16[1,1024,1024]{2,1,0:T(8,128)(2,1)} %param.8) | copy-start | bytes 6291460
  3.8 0.8 copy-start.2
  4.7 0.7 copy-start.3
  5.4 0.7 copy-start.4
  6.1 0.7 copy-start.5

commit v2 on v1

v2 whole, which is shorter than its diff:
```python
import functools

import jax
import jax.numpy as jnp
from jax import lax
from jax.experimental import pallas as pl
from jax.experimental.pallas import tpu as pltpu
from jax.sharding import PartitionSpec as P

F32 = jnp.float32
BF16 = jnp.bfloat16
HIGHEST = lax.Precision.HIGHEST
LAST = (((1,), (1,)), ((), ()))
PLAIN = (((1,), (0,)), ((), ()))
FIRST = (((0,), (0,)), ((), ()))
NRHS = 16
HALF = 512
WIDTH = 2 * HALF
FACE_CORNERS = 12
CORNERS = 768
PAYLOAD = 1024
BLOCKS = 4


def split(value, terms):
    parts = []
    for _ in range(terms):
        part = value.astype(BF16)
        parts.append(part)
        value = value - part.astype(F32)
    return parts


def narrow_dot(value, exact, dims, terms=3):
    rows = value.shape[0]
    stacked = jnp.concatenate(split(value, terms), axis=0)
    out = lax.dot_general(stacked, exact, dims, preferred_element_type=F32)
    total = out[:rows]
    for term in range(1, terms):
        total = total + out[term * rows : (term + 1) * rows]
    return total


def full_dot(left, right, dims):
    return lax.dot_general(left, right, dims, precision=HIGHEST, preferred_element_type=F32)


def symmetric_part(matrix):
    return 0.5 * (matrix + matrix.T)


def spd_solve(matrix, target):
    size = matrix.shape[0]
    both = jnp.concatenate([matrix, target], axis=1)
    rows = lax.broadcasted_iota(jnp.int32, both.shape, 0)
    for k in range(size):
        column = jnp.broadcast_to(both[:, k : k + 1], both.shape)
        pivot_row = both[k : k + 1, :] / column[k : k + 1, :]
        both = jnp.where(rows == k, pivot_row, both - column * pivot_row)
    return both[:, size:]


def kernel(
    blk_count, grp_count, ny, nz,
    rhs_hbm, prec_hbm, dual_hbm, couple_hbm, map_hbm, sign_hbm, inverse_hbm,
    mult_ref, resid_ref,
    rhs, prec, dual, couple, corner_map, signs, inverse, inverse_high, inverse_low,
    face_out, face_in, pieces, gathered, by_y, by_z, final, gram_spot, gram_y, gram_z,
    load_sem, prec_sem, face_send, face_recv,
    scatter_send, scatter_recv, y_send, y_recv, z_send, z_recv, final_send, final_recv,
    gram_send, gram_recv, gram_y_send, gram_y_recv, gram_z_send, gram_z_recv,
):
    small_loads = [
        pltpu.make_async_copy(source, target, load_sem.at[index])
        for index, (source, target) in enumerate(
            ((couple_hbm, couple), (map_hbm, corner_map), (rhs_hbm, rhs), (sign_hbm, signs))
        )
    ]
    block_rows = WIDTH // BLOCKS
    prec_loads = [
        pltpu.make_async_copy(
            prec_hbm.at[pl.ds(index * block_rows, block_rows)],
            prec.at[pl.ds(index * block_rows, block_rows)],
            prec_sem.at[index],
        )
        for index in range(BLOCKS)
    ]
    late_loads = [
        pltpu.make_async_copy(dual_hbm, dual, load_sem.at[4]),
        pltpu.make_async_copy(inverse_hbm, inverse, load_sem.at[5]),
    ]
    for load in small_loads + prec_loads:
        load.start()

    blk = lax.axis_index("blk")
    grp = lax.axis_index("grp")
    core = lax.rem(blk, 2)
    z = lax.rem(lax.div(blk, 2), nz)
    y = lax.div(blk, 2 * nz)
    spot = grp * 2 + core
    spots = 2 * grp_count
    lanes = PAYLOAD // spots

    def at(blk_index, grp_index):
        return {"blk": blk_index, "grp": grp_index}

    def spot_peer(step):
        other = lax.rem(spot + step, spots)
        return other, at(blk - core + lax.rem(other, 2), lax.div(other, 2))

    def y_peer(step):
        other = lax.rem(y + step, ny)
        return other, at(blk + (other - y) * (2 * nz), grp)

    def z_peer(step):
        other = lax.rem(z + step, nz)
        return other, at(blk + (other - z) * 2, grp)

    left = at(lax.rem(blk + blk_count - 1, blk_count), grp)
    right = at(lax.rem(blk + 1, blk_count), grp)

    barrier = pltpu.get_barrier_semaphore()
    greeted = [z_peer(step)[1] for step in range(1, nz)]
    greeted += [y_peer(step)[1] for step in range(1, ny)]
    greeted += [spot_peer(step)[1] for step in range(1, spots)]
    greeted += [left, right]
    for peer in greeted:
        pl.semaphore_signal(
            barrier, inc=1, device_id=peer, device_id_type=pl.DeviceIdType.MESH
        )

    def remote(source, target, send_sem, recv_sem, peer):
        return pltpu.make_async_remote_copy(
            src_ref=source,
            dst_ref=target,
            send_sem=send_sem,
            recv_sem=recv_sem,
            device_id=peer,
            device_id_type=pl.DeviceIdType.MESH,
        )

    def face_copies(turn):
        return (
            remote(
                face_out.at[turn, 0], face_in.at[turn, 1],
                face_send.at[turn, 0], face_recv.at[turn, 1], left,
            ),
            remote(
                face_out.at[turn, 1], face_in.at[turn, 0],
                face_send.at[turn, 1], face_recv.at[turn, 0], right,
            ),
        )

    def send_faces(turn, lower, upper):
        face_out[turn, 0] = lower
        face_out[turn, 1] = upper
        for copy in face_copies(turn):
            copy.start()

    def send_signed(turn, signed_out):
        send_faces(turn, signed_out[:, :HALF], signed_out[:, HALF:])

    def wait_faces(turn):
        for copy in face_copies(turn):
            copy.wait_recv()

    def take_faces(turn, signed_out):
        wait_faces(turn)
        partner = jnp.concatenate([face_in[turn, 0], face_in[turn, 1]], axis=1)
        return live * (signed_out + partner)

    drains = []

    def exchange(peer_of, count, own, source_of, buffer, send_sem, recv_sem):
        arrivals = []
        for step in range(1, count):
            other, peer = peer_of(step)
            send = remote(source_of(other), buffer.at[own], send_sem.at[other], recv_sem.at[own], peer)
            send.start()
            drains.append(send)
            arrivals.append(
                remote(source_of(other), buffer.at[other], send_sem.at[other], recv_sem.at[other], peer)
            )

        def arrive():
            for copy in arrivals:
                copy.wait_recv()

        return arrive

    def spread(peer_of, count, own, buffer, send_sem, recv_sem, value):
        buffer[own] = value
        return exchange(
            peer_of, count, own, lambda other: buffer.at[own], buffer, send_sem, recv_sem
        )

    def total_of(buffer, count):
        terms = [buffer[index] for index in range(count)]
        while len(terms) > 1:
            terms = [sum(terms[index : index + 2]) for index in range(0, len(terms), 2)]
        return terms[0]

    def padded(face_couple, face_map):
        size = NRHS - FACE_CORNERS
        block = jnp.concatenate([face_couple, jnp.zeros((size, HALF), F32)], axis=0)
        row = jnp.concatenate([face_map, jnp.zeros((1, HALF - FACE_CORNERS), F32)], axis=1)
        return jnp.where(block_row == FACE_CORNERS, row, block)

    def coupling_of(block):
        return jnp.where(block_row < FACE_CORNERS, block, 0.0)

    def onehot_of(block):
        row = jnp.broadcast_to(block[FACE_CORNERS : FACE_CORNERS + 1, :128], (NRHS, 128))
        column = jnp.sum(jnp.where(diagonal, row, 0.0), axis=1, keepdims=True)
        hit = jnp.logical_and(column == corner_lane, corner_row < FACE_CORNERS)
        return jnp.where(hit, 1.0, 0.0)

    block_row = lax.broadcasted_iota(jnp.int32, (NRHS, HALF), 0)
    corner_row = lax.broadcasted_iota(jnp.int32, (NRHS, CORNERS), 0)
    corner_lane = lax.broadcasted_iota(jnp.int32, (NRHS, CORNERS), 1).astype(F32)
    diagonal = lax.broadcasted_iota(jnp.int32, (NRHS, 128), 0) == lax.broadcasted_iota(
        jnp.int32, (NRHS, 128), 1
    )
    lane = lax.broadcasted_iota(jnp.int32, (1, WIDTH), 1)
    lower_live = jnp.where(blk > 0, 1.0, 0.0).astype(F32)
    upper_live = jnp.where(blk < blk_count - 1, 1.0, 0.0).astype(F32)
    live = jnp.where(lane < HALF, lower_live, upper_live)

    small_loads[0].wait()
    small_loads[1].wait()
    couple_all = couple[0].astype(F32)
    map_all = corner_map[...].astype(F32)
    own_lower = padded(couple_all[:FACE_CORNERS], map_all[:, :FACE_CORNERS])
    own_upper = padded(couple_all[FACE_CORNERS:], map_all[:, FACE_CORNERS:])
    pl.semaphore_wait(barrier, len(greeted))
    send_faces(0, own_lower, own_upper)

    small_loads[2].wait()
    small_loads[3].wait()
    face_sign = signs[...].astype(F32) * live
    residual = live * rhs[0]

    def prec_product(values, wait):
        rounded = (face_sign * values).astype(BF16)
        total = None
        for index in range(BLOCKS):
            if wait:
                prec_loads[index].wait()
            span = slice(index * block_rows, (index + 1) * block_rows)
            part = lax.dot_general(
                rounded[:, span], prec[span, :], PLAIN, preferred_element_type=F32
            )
            total = part if total is None else total + part
        return total

    local_out = prec_product(residual, True)
    for load in late_loads:
        load.start()
    send_signed(1, face_sign * local_out)

    wait_faces(0)
    across_lower = face_in[0, 0]
    across_upper = face_in[0, 1]
    zeros = jnp.zeros((NRHS, HALF), F32)
    coupling = jnp.concatenate(
        [
            jnp.concatenate([coupling_of(own_lower), zeros], axis=1),
            jnp.concatenate([zeros, coupling_of(own_upper)], axis=1),
            jnp.concatenate([-coupling_of(across_lower), zeros], axis=1),
            jnp.concatenate([zeros, -coupling_of(across_upper)], axis=1),
        ],
        axis=0,
    ).astype(BF16)
    onehot = jnp.concatenate(
        [onehot_of(block) for block in (own_lower, own_upper, across_lower, across_upper)], axis=0
    ).astype(BF16)

    def combine(weights, values):
        return full_dot(weights.T, values, PLAIN)

    def reduce_all(turn, local_out, meanwhile):
        signed_out = face_sign * local_out
        face_turn = 1 + 3 * turn
        partial = narrow_dot(live * local_out, coupling, LAST)
        corner = narrow_dot(partial, onehot, PLAIN)
        for index in range(spots):
            first = index * lanes
            pieces[turn, index] = (
                corner[:, first : first + lanes]
                if first < CORNERS
                else jnp.zeros((NRHS, lanes), F32)
            )
        scattered = exchange(
            spot_peer, spots, spot, lambda other: pieces.at[turn, other],
            gathered.at[turn], scatter_send.at[turn], scatter_recv.at[turn],
        )
        gathered[turn, spot] = pieces[turn, spot]
        precond = take_faces(face_turn, signed_out)
        signed_in = face_sign * precond
        if turn == 0:
            late_loads[0].wait()
        high, low = split(signed_in, 2)
        both = lax.dot_general(
            jnp.concatenate([high, low], axis=0), dual[...], PLAIN, preferred_element_type=F32
        )
        product, correction = both[:NRHS], both[NRHS:]
        scattered()
        along_y = spread(
            y_peer, ny, y, by_y.at[turn], y_send.at[turn], y_recv.at[turn],
            total_of(gathered.at[turn], spots),
        )
        grams = [
            full_dot(residual, precond, LAST),
            2.0 * full_dot(signed_in, product, LAST),
            2.0 * full_dot(signed_in, product if turn == 0 else product_old, LAST),
            jnp.zeros((NRHS, NRHS), F32),
        ]
        wide = jnp.concatenate(grams, axis=1)
        packed = jnp.concatenate([wide[:8], wide[8:]], axis=1)
        gram_at_spot = spread(
            spot_peer, spots, spot, gram_spot.at[turn], gram_send.at[turn], gram_recv.at[turn], packed
        )
        send_signed(face_turn + 1, face_sign * product)
        send_signed(face_turn + 2, face_sign * correction)
        along_y()
        along_z = spread(
            z_peer, nz, z, by_z.at[turn], z_send.at[turn], z_recv.at[turn],
            total_of(by_y.at[turn], ny),
        )
        gram_at_spot()
        gram_along_y = spread(
            y_peer, ny, y, gram_y.at[turn], gram_y_send.at[turn], gram_y_recv.at[turn],
            total_of(gram_spot.at[turn], spots),
        )
        between = meanwhile()
        gram_along_y()
        gram_along_z = spread(
            z_peer, nz, z, gram_z.at[turn], gram_z_send.at[turn], gram_z_recv.at[turn],
            total_of(gram_y.at[turn], ny),
        )
        along_z()
        gathered_back = spread(
            spot_peer, spots, spot, final.at[turn], final_send.at[turn], final_recv.at[turn],
            total_of(by_z.at[turn], nz),
        )
        image = take_faces(face_turn + 1, face_sign * product)
        correction = take_faces(face_turn + 2, face_sign * correction)
        gathered_back()
        corner = jnp.concatenate([final[turn, index] for index in range(spots)], axis=1)

        def take_grams():
            gram_along_z()
            total = total_of(gram_z.at[turn], nz)
            wide = jnp.concatenate([total[:, :64], total[:, 64:]], axis=0)
            return [wide[:, index * NRHS : (index + 1) * NRHS] for index in range(3)]

        return precond, product, image, correction, corner[:, :CORNERS], take_grams, between

    def prepare():
        late_loads[1].wait()
        high, middle, low = split(inverse[...], 3)
        inverse_high[...] = high
        inverse_low[...] = middle
        picked = lax.dot_general(onehot, high, PLAIN, preferred_element_type=F32)
        picked = picked + lax.dot_general(onehot, middle, PLAIN, preferred_element_type=F32)
        return picked + lax.dot_general(onehot, low, PLAIN, preferred_element_type=F32)

    def solve_corners(values):
        high, low = split(values, 2)
        both = lax.dot_general(
            jnp.concatenate([high, low], axis=0), inverse_high[...], PLAIN,
            preferred_element_type=F32,
        )
        cross = lax.dot_general(high, inverse_low[...], PLAIN, preferred_element_type=F32)
        return both[:NRHS] + (both[NRHS:] + cross)

    def coarse_image(corner):
        picked = full_dot(corner, inverse_rows, LAST)
        return face_sign * narrow_dot(picked, coupling, PLAIN)

    product_old = None
    direction, product_old, image_old, correction_old, corner_old, take_grams, inverse_rows = (
        reduce_all(0, local_out, prepare)
    )
    solved_old = solve_corners(corner_old)
    curve_coarse = 2.0 * full_dot(corner_old, solved_old, LAST)
    image_old = image_old + coarse_image(corner_old)
    gram_old, curve_old, _ = take_grams()
    curve_old = symmetric_part(curve_old + curve_coarse)
    alpha_old = spd_solve(curve_old, gram_old)
    residual = residual - combine(alpha_old, image_old)
    local_out = prec_product(residual, False)
    send_signed(4, face_sign * local_out)
    image_old = image_old + correction_old

    def invert():
        unit = lax.broadcasted_iota(jnp.int32, (NRHS, NRHS), 0) == lax.broadcasted_iota(
            jnp.int32, (NRHS, NRHS), 1
        )
        return spd_solve(symmetric_part(gram_old), jnp.where(unit, 1.0, 0.0).astype(F32))

    precond, _, image, correction, corner_new, take_grams, gram_inverse = reduce_all(
        1, local_out, invert
    )
    solved_new = solve_corners(corner_new)
    curve_coarse = 2.0 * full_dot(corner_new, solved_new, LAST)
    cross_coarse = 2.0 * full_dot(corner_new, solved_old, LAST)
    image = image + correction + coarse_image(corner_new)
    gram_new, curve_new, cross = take_grams()
    beta = full_dot(gram_inverse, gram_new, PLAIN)
    mixed = full_dot(cross + cross_coarse, beta, PLAIN)
    quadratic = full_dot(beta.T, full_dot(curve_old, beta, PLAIN), PLAIN)
    curve = symmetric_part(curve_new + curve_coarse + 2.0 * mixed + quadratic)
    alpha = spd_solve(curve, gram_new)
    through = full_dot(beta, alpha, PLAIN)
    mult_ref[0] = combine(
        jnp.concatenate([alpha_old + through, alpha], axis=0),
        jnp.concatenate([direction, precond], axis=0),
    )
    resid_ref[0] = residual - combine(
        jnp.concatenate([through, alpha], axis=0), jnp.concatenate([image_old, image], axis=0)
    )
    for copy in drains:
        copy.wait_send()
    for turn in range(7):
        for copy in face_copies(turn):
            copy.wait_send()


def extents(blk_count):
    return {192: (8, 12), 8: (2, 2)}[blk_count]


def solution(mesh):
    blk_count, grp_count = mesh.shape["blk"], mesh.shape["grp"]
    ny, nz = extents(blk_count)
    spots = 2 * grp_count
    piece = (NRHS, PAYLOAD // spots)
    dma = pltpu.SemaphoreType.DMA
    in_vmem = pl.BlockSpec(memory_space=pltpu.VMEM)
    in_place = pl.BlockSpec(memory_space=pl.ANY)

    def local(dual_rhs, dual_ops, prec_ops, corner_coupling, corner_map, signs, coarse_inverse):
        result = jax.ShapeDtypeStruct((1, NRHS, WIDTH), F32)
        return pl.pallas_call(
            functools.partial(kernel, blk_count, grp_count, ny, nz),
            out_shape=(result, result),
            in_specs=[in_place] * 7,
            out_specs=(in_vmem, in_vmem),
            scratch_shapes=[
                pltpu.VMEM((1, NRHS, WIDTH), F32),
                pltpu.VMEM((WIDTH, WIDTH), BF16),
                pltpu.VMEM((WIDTH, WIDTH), BF16),
                pltpu.VMEM((1, 2 * FACE_CORNERS, HALF), BF16),
                pltpu.VMEM((1, 2 * FACE_CORNERS), jnp.int32),
                pltpu.VMEM((1, WIDTH), jnp.int32),
                pltpu.VMEM((CORNERS, CORNERS), F32),
                pltpu.VMEM((CORNERS, CORNERS), BF16),
                pltpu.VMEM((CORNERS, CORNERS), BF16),
                pltpu.VMEM((7, 2, NRHS, HALF), F32),
                pltpu.VMEM((7, 2, NRHS, HALF), F32),
                pltpu.VMEM((2, spots, *piece), F32),
                pltpu.VMEM((2, spots, *piece), F32),
                pltpu.VMEM((2, ny, *piece), F32),
                pltpu.VMEM((2, nz, *piece), F32),
                pltpu.VMEM((2, spots, *piece), F32),
                pltpu.VMEM((2, spots, 8, 128), F32),
                pltpu.VMEM((2, ny, 8, 128), F32),
                pltpu.VMEM((2, nz, 8, 128), F32),
                dma((6,)),
                dma((BLOCKS,)),
                dma((7, 2)),
                dma((7, 2)),
                *[dma((2, count)) for count in (spots, ny, nz, spots, spots, ny, nz) for _ in range(2)],
            ],
            compiler_params=pltpu.CompilerParams(
                collective_id=0, has_side_effects=True, vmem_limit_bytes=67043328
            ),
            name="block_conjugate_gradients",
        )(
            dual_rhs, prec_ops.reshape(WIDTH, WIDTH), dual_ops.reshape(WIDTH, WIDTH),
            corner_coupling, corner_map, signs, coarse_inverse,
        )

    in_specs = (
        P("grp", None, "blk"),
        P("grp", "blk", None),
        P("grp", "blk", None),
        P("grp", "blk", None),
        P("grp", "blk"),
        P("grp", "blk"),
        P(),
    )
    out_specs = (P("grp", None, "blk"), P("grp", None, "blk"))
    return jax.shard_map(local, mesh=mesh, in_specs=in_specs, out_specs=out_specs, check_vma=False)
```

time: 87.6 us -> 78.3 us (0.89)
  Pallas kernels: 79.2 us -> 74.4 us
  local copies, waits for them, and re-layouts: 7.35 us -> 2.95 us
    pallas_call x1, Pallas kernels: 79.2 us -> 74.4 us  [local(): pl.pallas_call(functools.partial(kernel, blk_count, grp_count, ny, nz), o...]
    unnamed x14 -> x2, local copies, waits for them, and re-layouts: 7.35 us -> 2.95 us
where the time goes in v2:
time: 78.3 us; the launch traced here: 78 us
  Pallas kernels  74.4 us (95%)
  local copies, waits for them, and re-layouts  2.95 us (4%)
    pallas_call x1, Pallas kernels, local(): pl.pallas_call(functools.partial(kernel, blk_count, grp_count, ny, nz), o...  74.4 us
    unnamed x2, local copies, waits for them, and re-layouts  2.95 us

profile of v2, /device:TPU:1, one launch (start us, length us, event | category | flops | bytes accessed | tf_op | source)
XLA Modules:
  0.0 78.0 jit_solution(14031661905602256995)
XLA Ops:
  0.6 74.4 %block_conjugate_gradients.1 = (f32[1,16,1024]{2,1,0:T(8,128)}, f32[1,16,1024]{2,1,0:T(8,128)}) custom-call(f32[1,16,1024]{2,1,0:T(8,128)} %rhs_hbm.1, bf16[1024,1024]{1,0:T(8,128)(2,1)} %bitcast.2, bf16[1024,1024]{1,0:T(8,128)(2,1)} %bitcast.3, bf16[1,24,512]{2,1,0:T(8,128)(2,1)} %couple_hbm.1, s32[1,24]{1,0:T(1,128)} %map_hbm.1, s32[1,1024]{1,0:T(1,128)} %sign_hbm.1, ...), custom_call_target="tpu_custom_call" | custom-call | tf_op jit(solution)/shard_map/block_conjugate_gradients/pallas_call | solution.py:445
  75.1 1.5 %copy.11 = f32[1,16,1024]{2,1,0:T(8,128)} copy(f32[1,16,1024]{2,1,0:T(8,128)} %get-tuple-element.4) | data formatting | bytes 131072
  76.6 1.5 %copy.12 = f32[1,16,1024]{2,1,0:T(8,128)} copy(f32[1,16,1024]{2,1,0:T(8,128)} %get-tuple-element.5) | data formatting | bytes 131072

commit v3 on v2

--- a/solution.py
+++ b/solution.py
@@ -18,8 +18,9 @@
 WIDTH = 2 * HALF
 FACE_CORNERS = 12
 CORNERS = 768
-PAYLOAD = 1024
 BLOCKS = 4
+TURNS = 6
+CORRECTION = 5
 
 
 def split(value, terms):
@@ -43,6 +44,40 @@
 
 def full_dot(left, right, dims):
     return lax.dot_general(left, right, dims, precision=HIGHEST, preferred_element_type=F32)
+
+
+def to_pieces(corner, spots):
+    tiles = [
+        corner[8 * (index % 2) : 8 * (index % 2) + 8, 128 * (index // 2) : 128 * (index // 2) + 128]
+        for index in range(NRHS * CORNERS // 1024)
+    ]
+    share = len(tiles) * 8 // spots
+    if share % 8 == 0:
+        many = share // 8
+        return [
+            jnp.concatenate(tiles[index * many : (index + 1) * many], axis=0)
+            for index in range(spots)
+        ]
+    pieces = []
+    for index in range(0, len(tiles), 3):
+        first, middle, last = tiles[index : index + 3]
+        pieces.append(jnp.concatenate([first, middle[:4]], axis=0))
+        pieces.append(jnp.concatenate([last, middle[4:]], axis=0))
+    return pieces
+
+
+def from_pieces(pieces):
+    tiles = []
+    if pieces[0].shape[0] % 8 == 0:
+        for piece in pieces:
+            tiles += [piece[index : index + 8] for index in range(0, piece.shape[0], 8)]
+    else:
+        for first, last in zip(pieces[::2], pieces[1::2]):
+            tiles += [first[:8], jnp.concatenate([first[8:], last[8:]], axis=0), last[:8]]
+    columns = [
+        jnp.concatenate(tiles[index : index + 2], axis=0) for index in range(0, len(tiles), 2)
+    ]
+    return jnp.concatenate(columns, axis=1)
 
 
 def symmetric_part(matrix):
@@ -63,7 +98,7 @@
 def kernel(
     blk_count, grp_count, ny, nz,
     rhs_hbm, prec_hbm, dual_hbm, couple_hbm, map_hbm, sign_hbm, inverse_hbm,
-    mult_ref, resid_ref,
+    out_ref,
     rhs, prec, dual, couple, corner_map, signs, inverse, inverse_high, inverse_low,
     face_out, face_in, pieces, gathered, by_y, by_z, final, gram_spot, gram_y, gram_z,
     load_sem, prec_sem, face_send, face_recv,
@@ -99,7 +134,6 @@
     y = lax.div(blk, 2 * nz)
     spot = grp * 2 + core
     spots = 2 * grp_count
-    lanes = PAYLOAD // spots
 
     def at(blk_index, grp_index):
         return {"blk": blk_index, "grp": grp_index}
@@ -280,22 +314,22 @@
 
     def reduce_all(turn, local_out, meanwhile):
         signed_out = face_sign * local_out
-        face_turn = 1 + 3 * turn
+        face_turn = 1 + 2 * turn
         partial = narrow_dot(live * local_out, coupling, LAST)
         corner = narrow_dot(partial, onehot, PLAIN)
-        for index in range(spots):
-            first = index * lanes
-            pieces[turn, index] = (
-                corner[:, first : first + lanes]
-                if first < CORNERS
-                else jnp.zeros((NRHS, lanes), F32)
-            )
+        for index, piece in enumerate(to_pieces(corner, spots)):
+            pieces[turn, index] = piece
         scattered = exchange(
             spot_peer, spots, spot, lambda other: pieces.at[turn, other],
             gathered.at[turn], scatter_send.at[turn], scatter_recv.at[turn],
         )
         gathered[turn, spot] = pieces[turn, spot]
         precond = take_faces(face_turn, signed_out)
+        scattered()
+        along_y = spread(
+            y_peer, ny, y, by_y.at[turn], y_send.at[turn], y_recv.at[turn],
+            total_of(gathered.at[turn], spots),
+        )
         signed_in = face_sign * precond
         if turn == 0:
             late_loads[0].wait()
@@ -304,11 +338,6 @@
             jnp.concatenate([high, low], axis=0), dual[...], PLAIN, preferred_element_type=F32
         )
         product, correction = both[:NRHS], both[NRHS:]
-        scattered()
-        along_y = spread(
-            y_peer, ny, y, by_y.at[turn], y_send.at[turn], y_recv.at[turn],
-            total_of(gathered.at[turn], spots),
-        )
         grams = [
             full_dot(residual, precond, LAST),
             2.0 * full_dot(signed_in, product, LAST),
@@ -320,8 +349,8 @@
         gram_at_spot = spread(
             spot_peer, spots, spot, gram_spot.at[turn], gram_send.at[turn], gram_recv.at[turn], packed
         )
-        send_signed(face_turn + 1, face_sign * product)
-        send_signed(face_turn + 2, face_sign * correction)
+        product_out = face_sign * (product if turn == 0 else product + correction)
+        send_signed(face_turn + 1, product_out)
         along_y()
         along_z = spread(
             z_peer, nz, z, by_z.at[turn], z_send.at[turn], z_recv.at[turn],
@@ -343,10 +372,11 @@
             spot_peer, spots, spot, final.at[turn], final_send.at[turn], final_recv.at[turn],
             total_of(by_z.at[turn], nz),
         )
-        image = take_faces(face_turn + 1, face_sign * product)
-        correction = take_faces(face_turn + 2, face_sign * correction)
+        if turn == 0:
+            send_signed(CORRECTION, face_sign * correction)
+        image = take_faces(face_turn + 1, product_out)
         gathered_back()
-        corner = jnp.concatenate([final[turn, index] for index in range(spots)], axis=1)
+        corner = from_pieces([final[turn, index] for index in range(spots)])
 
         def take_grams():
             gram_along_z()
@@ -354,7 +384,7 @@
             wide = jnp.concatenate([total[:, :64], total[:, 64:]], axis=0)
             return [wide[:, index * NRHS : (index + 1) * NRHS] for index in range(3)]
 
-        return precond, product, image, correction, corner[:, :CORNERS], take_grams, between
+        return precond, product, image, face_sign * correction, corner, take_grams, between
 
     def prepare():
         late_loads[1].wait()
@@ -390,63 +420,67 @@
     alpha_old = spd_solve(curve_old, gram_old)
     residual = residual - combine(alpha_old, image_old)
     local_out = prec_product(residual, False)
-    send_signed(4, face_sign * local_out)
-    image_old = image_old + correction_old
+    send_signed(3, face_sign * local_out)
 
     def invert():
         unit = lax.broadcasted_iota(jnp.int32, (NRHS, NRHS), 0) == lax.broadcasted_iota(
             jnp.int32, (NRHS, NRHS), 1
         )
-        return spd_solve(symmetric_part(gram_old), jnp.where(unit, 1.0, 0.0).astype(F32))
-
-    precond, _, image, correction, corner_new, take_grams, gram_inverse = reduce_all(
-        1, local_out, invert
+        inverted = spd_solve(symmetric_part(gram_old), jnp.where(unit, 1.0, 0.0).astype(F32))
+        return inverted, full_dot(inverted, full_dot(curve_old, inverted, PLAIN), PLAIN)
+
+    precond, _, image, _, corner_new, take_grams, (gram_inverse, weight) = (
+        reduce_all(1, local_out, invert)
     )
     solved_new = solve_corners(corner_new)
     curve_coarse = 2.0 * full_dot(corner_new, solved_new, LAST)
     cross_coarse = 2.0 * full_dot(corner_new, solved_old, LAST)
-    image = image + correction + coarse_image(corner_new)
+    image = image + coarse_image(corner_new)
+    image_old = image_old + take_faces(CORRECTION, correction_old)
     gram_new, curve_new, cross = take_grams()
     beta = full_dot(gram_inverse, gram_new, PLAIN)
-    mixed = full_dot(cross + cross_coarse, beta, PLAIN)
-    quadratic = full_dot(beta.T, full_dot(curve_old, beta, PLAIN), PLAIN)
-    curve = symmetric_part(curve_new + curve_coarse + 2.0 * mixed + quadratic)
+    inner = full_dot(
+        jnp.concatenate([2.0 * (cross + cross_coarse), gram_new.T], axis=1),
+        jnp.concatenate([gram_inverse, weight], axis=0),
+        PLAIN,
+    )
+    curve = symmetric_part(curve_new + curve_coarse + full_dot(inner, gram_new, PLAIN))
     alpha = spd_solve(curve, gram_new)
     through = full_dot(beta, alpha, PLAIN)
-    mult_ref[0] = combine(
+    out_ref[0] = combine(
         jnp.concatenate([alpha_old + through, alpha], axis=0),
         jnp.concatenate([direction, precond], axis=0),
     )
-    resid_ref[0] = residual - combine(
+    out_ref[1] = residual - combine(
         jnp.concatenate([through, alpha], axis=0), jnp.concatenate([image_old, image], axis=0)
     )
     for copy in drains:
         copy.wait_send()
-    for turn in range(7):
+    for turn in range(TURNS):
         for copy in face_copies(turn):
             copy.wait_send()
 
 
 def extents(blk_count):
-    return {192: (8, 12), 8: (2, 2)}[blk_count]
+    return {192: (8, 12), 8: (2, 2), 4: (1, 2)}[blk_count]
 
 
 def solution(mesh):
     blk_count, grp_count = mesh.shape["blk"], mesh.shape["grp"]
     ny, nz = extents(blk_count)
     spots = 2 * grp_count
-    piece = (NRHS, PAYLOAD // spots)
+    piece = (NRHS * CORNERS // 128 // spots, 128)
     dma = pltpu.SemaphoreType.DMA
     in_vmem = pl.BlockSpec(memory_space=pltpu.VMEM)
     in_place = pl.BlockSpec(memory_space=pl.ANY)
 
     def local(dual_rhs, dual_ops, prec_ops, corner_coupling, corner_map, signs, coarse_inverse):
         result = jax.ShapeDtypeStruct((1, NRHS, WIDTH), F32)
-        return pl.pallas_call(
+        both = pl.pallas_call(
             functools.partial(kernel, blk_count, grp_count, ny, nz),
-            out_shape=(result, result),
+            out_shape=jax.ShapeDtypeStruct((2, NRHS, WIDTH), F32),
             in_specs=[in_place] * 7,
-            out_specs=(in_vmem, in_vmem),
+            out_specs=in_vmem,
             scratch_shapes=[
                 pltpu.VMEM((1, NRHS, WIDTH), F32),
                 pltpu.VMEM((WIDTH, WIDTH), BF16),
@@ -457,8 +491,8 @@
                 pltpu.VMEM((CORNERS, CORNERS), F32),
                 pltpu.VMEM((CORNERS, CORNERS), BF16),
                 pltpu.VMEM((CORNERS, CORNERS), BF16),
-                pltpu.VMEM((7, 2, NRHS, HALF), F32),
-                pltpu.VMEM((7, 2, NRHS, HALF), F32),
+                pltpu.VMEM((TURNS, 2, NRHS, HALF), F32),
+                pltpu.VMEM((TURNS, 2, NRHS, HALF), F32),
                 pltpu.VMEM((2, spots, *piece), F32),
                 pltpu.VMEM((2, spots, *piece), F32),
                 pltpu.VMEM((2, ny, *piece), F32),
@@ -469,8 +503,8 @@
                 pltpu.VMEM((2, nz, 8, 128), F32),
                 dma((6,)),
                 dma((BLOCKS,)),
-                dma((7, 2)),
-                dma((7, 2)),
+                dma((TURNS, 2)),
+                dma((TURNS, 2)),
                 *[dma((2, count)) for count in (spots, ny, nz, spots, spots, ny, nz) for _ in range(2)],
             ],
             compiler_params=pltpu.CompilerParams(
@@ -481,6 +515,7 @@
             dual_rhs, prec_ops.reshape(WIDTH, WIDTH), dual_ops.reshape(WIDTH, WIDTH),
             corner_coupling, corner_map, signs, coarse_inverse,
         )
+        return both[:1], both[1:]
 
     in_specs = (
         P("grp", None, "blk"),

time: 78.3 us -> 73.8 us (0.943)
  Pallas kernels: 74.4 us -> 71.5 us
  local copies, waits for them, and re-layouts: 2.95 us -> 1.53 us
    pallas_call x1, Pallas kernels: 74.4 us -> 71.5 us  [local(): pl.pallas_call(functools.partial(kernel, blk_count, grp_count, ny, nz), o...]
    unnamed x2 -> x0, local copies, waits for them, and re-layouts: 2.95 us -> none
    slice x0 -> x1, local copies, waits for them, and re-layouts: none -> 1.53 us  [local(): return (both[:1], both[1:])]
where the time goes in v3:
time: 73.8 us; the launch traced here: 73.6 us
  Pallas kernels  71.5 us (97%)
  local copies, waits for them, and re-layouts  1.53 us (2%)
    pallas_call x1, Pallas kernels, local(): pl.pallas_call(functools.partial(kernel, blk_count, grp_count, ny, nz), o...  71.5 us
    slice x1, local copies, waits for them, and re-layouts, local(): return (both[:1], both[1:])  1.53 us

profile of v3, /device:TPU:1, one launch (start us, length us, event | category | flops | bytes accessed | tf_op | source)
XLA Modules:
  0.0 73.6 jit_solution(8176670698040084413)
XLA Ops:
  0.6 71.5 %block_conjugate_gradients.1 = f32[2,16,1024]{2,1,0:T(8,128)} custom-call(f32[1,16,1024]{2,1,0:T(8,128)} %rhs_hbm.1, bf16[1024,1024]{1,0:T(8,128)(2,1)} %bitcast.2, bf16[1024,1024]{1,0:T(8,128)(2,1)} %bitcast.3, bf16[1,24,512]{2,1,0:T(8,128)(2,1)} %couple_hbm.1, s32[1,24]{1,0:T(1,128)} %map_hbm.1, s32[1,1024]{1,0:T(1,128)} %sign_hbm.1, f32[768,768]{1,0:T(8,128)} %inverse_hbm.1), custom_call_target="tpu_custom_call" | custom-call | tf_op jit(solution)/shard_map/block_conjugate_gradients/pallas_call | solution.py:479
  72.1 1.5 %fusion = (f32[1,16,1024]{2,1,0:T(8,128)}, f32[1,16,1024]{2,1,0:T(8,128)}) fusion(f32[2,16,1024]{2,1,0:T(8,128)} %block_conjugate_gradients.1), kind=kLoop, calls=%fused_computation | loop fusion | bytes 262144 | tf_op jit(solution)/shard_map/slice | solution.py:518

commit v4 on v3

--- a/solution.py
+++ b/solution.py
@@ -338,12 +338,9 @@
             jnp.concatenate([high, low], axis=0), dual[...], PLAIN, preferred_element_type=F32
         )
         product, correction = both[:NRHS], both[NRHS:]
-        grams = [
-            full_dot(residual, precond, LAST),
-            2.0 * full_dot(signed_in, product, LAST),
-            2.0 * full_dot(signed_in, product if turn == 0 else product_old, LAST),
-            jnp.zeros((NRHS, NRHS), F32),
-        ]
+        others = product if turn == 0 else jnp.concatenate([product, product_old], axis=0)
+        grams = [full_dot(residual, precond, LAST), 2.0 * full_dot(signed_in, others, LAST)]
+        grams.append(jnp.zeros((NRHS, 4 * NRHS - NRHS - others.shape[0]), F32))
         wide = jnp.concatenate(grams, axis=1)
         packed = jnp.concatenate([wide[:8], wide[8:]], axis=1)
         gram_at_spot = spread(
@@ -388,12 +385,9 @@
 
     def prepare():
         late_loads[1].wait()
-        high, middle, low = split(inverse[...], 3)
+        high, low = split(inverse[...], 2)
         inverse_high[...] = high
-        inverse_low[...] = middle
-        picked = lax.dot_general(onehot, high, PLAIN, preferred_element_type=F32)
-        picked = picked + lax.dot_general(onehot, middle, PLAIN, preferred_element_type=F32)
-        return picked + lax.dot_general(onehot, low, PLAIN, preferred_element_type=F32)
+        inverse_low[...] = low
 
     def solve_corners(values):
         high, low = split(values, 2)
@@ -404,17 +398,17 @@
         cross = lax.dot_general(high, inverse_low[...], PLAIN, preferred_element_type=F32)
         return both[:NRHS] + (both[NRHS:] + cross)
 
-    def coarse_image(corner):
-        picked = full_dot(corner, inverse_rows, LAST)
+    def coarse_image(solved):
+        picked = narrow_dot(solved, onehot, LAST)
         return face_sign * narrow_dot(picked, coupling, PLAIN)
 
     product_old = None
-    direction, product_old, image_old, correction_old, corner_old, take_grams, inverse_rows = (
+    direction, product_old, image_old, correction_old, corner_old, take_grams, _ = (
         reduce_all(0, local_out, prepare)
     )
     solved_old = solve_corners(corner_old)
     curve_coarse = 2.0 * full_dot(corner_old, solved_old, LAST)
-    image_old = image_old + coarse_image(corner_old)
+    image_old = image_old + coarse_image(solved_old)
     gram_old, curve_old, _ = take_grams()
     curve_old = symmetric_part(curve_old + curve_coarse)
     alpha_old = spd_solve(curve_old, gram_old)
@@ -435,7 +429,7 @@
     solved_new = solve_corners(corner_new)
     curve_coarse = 2.0 * full_dot(corner_new, solved_new, LAST)
     cross_coarse = 2.0 * full_dot(corner_new, solved_old, LAST)
-    image = image + coarse_image(corner_new)
+    image = image + coarse_image(solved_new)
     image_old = image_old + take_faces(CORRECTION, correction_old)
     gram_new, curve_new, cross = take_grams()
     beta = full_dot(gram_inverse, gram_new, PLAIN)

time: 73.8 us -> 73.2 us (level)
  no operation moved by 1% of the time
where the time goes in v4:
time: 73.2 us; the launch traced here: 73 us
  Pallas kernels  70.9 us (97%)
  local copies, waits for them, and re-layouts  1.53 us (2%)
    pallas_call x1, Pallas kernels, local(): pl.pallas_call(functools.partial(kernel, blk_count, grp_count, ny, nz), o...  70.9 us
    slice x1, local copies, waits for them, and re-layouts, local(): return (both[:1], both[1:])  1.53 us

profile of v4, /device:TPU:1, one launch (start us, length us, event | category | flops | bytes accessed | tf_op | source)
XLA Modules:
  0.0 73.0 jit_solution(11236313147972625181)
XLA Ops:
  0.6 70.9 %block_conjugate_gradients.1 = f32[2,16,1024]{2,1,0:T(8,128)} custom-call(f32[1,16,1024]{2,1,0:T(8,128)} %rhs_hbm.1, bf16[1024,1024]{1,0:T(8,128)(2,1)} %bitcast.2, bf16[1024,1024]{1,0:T(8,128)(2,1)} %bitcast.3, bf16[1,24,512]{2,1,0:T(8,128)(2,1)} %couple_hbm.1, s32[1,24]{1,0:T(1,128)} %map_hbm.1, s32[1,1024]{1,0:T(1,128)} %sign_hbm.1, f32[768,768]{1,0:T(8,128)} %inverse_hbm.1), custom_call_target="tpu_custom_call" | custom-call | tf_op jit(solution)/shard_map/block_conjugate_gradients/pallas_call | solution.py:473
  71.5 1.5 %fusion = (f32[1,16,1024]{2,1,0:T(8,128)}, f32[1,16,1024]{2,1,0:T(8,128)}) fusion(f32[2,16,1024]{2,1,0:T(8,128)} %block_conjugate_gradients.1), kind=kLoop, calls=%fused_computation | loop fusion | bytes 262144 | tf_op jit(solution)/shard_map/slice | solution.py:512
